TPU v7x, 32 devices: a whole 2x2x4 slice. The times are simulated.
32 devices in a mesh: group: 2 (over y), ctx: 4 (over z), smp: 2 (over x), head: 2 (over core).
Axes of the slice: x: 2, y: 2, z: 4, core: 2. Of those that a mesh axis runs over, the one named last changes fastest.
Arguments:
- queries: bfloat16 [512, 2, 4096], P(('group', 'smp'), 'head'), parts along dimension 0, may hold values from -8 to 8
- prefix_cache: bfloat16 [2, 8192, 2, 512], P(None, ('group', 'ctx'), 'head'), parts along dimension 1, may hold values from -8 to 8
- suffix_cache: bfloat16 [2, 512, 128, 2, 512], P(None, ('group', 'ctx', 'smp'), None, 'head'), parts along dimension 1, may hold values from -8 to 8
- suffix_length: int32 [512], P(('group', 'smp')), parts along dimension 0, may hold values from 1 to 128, as said below
- cache_sample: int32 [512], P('group'), parts along dimension 0, may hold values from 0 to 255, as said below
- residual: bfloat16 [512, 8192], P(('group', 'ctx', 'head'), 'smp'), parts along dimension 0, may hold values from -6 to 6
- w_out: bfloat16 [2, 4096, 8192], P('head', 'ctx', 'smp'), may hold values from -0.75 to 0.75
- norm_gain: float32 [8192], P('smp'), may hold values from 0.1 to 1.9
- gate_matrix: bfloat16 [8192, 16384], P('smp', ('ctx', 'head')), may hold values from -0.0625 to 0.0625
- w_up: bfloat16 [8192, 16384], P('smp', ('ctx', 'head')), may hold values from -0.0625 to 0.0625
- w_down: bfloat16 [16384, 8192], P(('ctx', 'head'), 'smp'), may hold values from -0.046875 to 0.046875
Outputs:
- mixed: bfloat16 [512, 8192], P(('group', 'ctx', 'head'), 'smp'), parts along dimension 0
There are 2 independent parts, one for each index of `group`. A program takes and returns all parts, laid end to end along the dimension named above; an argument that names none is the same for every part. Nothing has to cross between parts.
Inputs may be any that keep to these rules, and one draw needn't show every extreme that they name: `suffix_length`: the longest is exactly 128 in every draw. A permutation; cache row r and sample cache_sample[r] lie in the same group, the group of row r being (r // 32) % (2) and that of sample i being i // 128.
All inputs are finite; a program needn't handle non-finite values.
Results may differ from a plain program's by a relative error of at most 0.012.
Values may be sent and summed in bfloat16 or wider, within the bound.
A program may use at most 192 MiB of HBM per device.

v0:
```python
import jax
import jax.numpy as jnp
from jax import lax
from jax.sharding import PartitionSpec as P

D = 8192
QUERY_HEADS = 64
KEY_VALUE_HEADS = 8
HD = 128
EPSILON = 1e-05


def suffix_piece(row_queries, suffix_cache, row_lengths, key_value_heads_here, score_scale):
    rows_here = suffix_cache.shape[1]
    suffix_keys = suffix_cache[0].reshape(rows_here, -1, key_value_heads_here, HD)
    suffix_values = suffix_cache[1].reshape(rows_here, -1, key_value_heads_here, HD)
    row_scores = (
        jnp.einsum("rjgd,rtjd->rjgt", row_queries, suffix_keys, preferred_element_type=jnp.float32)
        * score_scale
    )
    positions = lax.broadcasted_iota(jnp.int32, row_scores.shape, 3)
    row_scores = jnp.where(positions < row_lengths[:, None, None, None], row_scores, -jnp.inf)
    row_high = jnp.max(row_scores, axis=3)
    row_weights = jnp.exp(row_scores - row_high[..., None])
    row_totals = jnp.sum(row_weights, axis=3)
    row_summed = jnp.einsum(
        "rjgt,rtjd->rjgd",
        row_weights.astype(jnp.bfloat16),
        suffix_values,
        preferred_element_type=jnp.float32,
    )
    row_output = (row_summed / row_totals[..., None]).astype(jnp.bfloat16)
    return (row_output, row_high + jnp.log(row_totals))


def merge_pieces(pieces):
    piece_values, piece_lse = pieces
    item_count = piece_values.shape[0]
    peak = jnp.max(piece_lse, axis=1, keepdims=True)
    piece_weights = jnp.exp(piece_lse - peak)
    shaped = piece_values.reshape(item_count, piece_values.shape[1], piece_lse.shape[2], HD)
    numer = jnp.sum(piece_weights[..., None] * shaped, axis=1)
    denom = jnp.sum(piece_weights, axis=1)
    return (numer / denom[..., None]).reshape(item_count, -1).astype(jnp.bfloat16)


def activate(gate_sum, up_sum, square_sum):
    factor = lax.rsqrt(square_sum / D + EPSILON)[:, None]
    return (jax.nn.silu(factor * gate_sum) * (factor * up_sum)).astype(jnp.bfloat16)


def on_device(
    queries,
    prefix_cache,
    suffix_cache,
    suffix_length,
    cache_sample,
    residual,
    w_out,
    norm_gain,
    gate_matrix,
    w_up,
    w_down,
):
    group_rows = queries.shape[0]
    key_value_heads_here = prefix_cache.shape[3] // HD
    queries_per_key_value = QUERY_HEADS // KEY_VALUE_HEADS
    heads_local = key_value_heads_here * queries_per_key_value
    score_scale = HD ** (-0.5)
    queries_split = queries.reshape(group_rows, key_value_heads_here, queries_per_key_value, HD)
    prefix_keys = prefix_cache[0].reshape(-1, key_value_heads_here, HD)
    prefix_values = prefix_cache[1].reshape(-1, key_value_heads_here, HD)
    scores = (
        jnp.einsum("sjgd,pjd->jsgp", queries_split, prefix_keys, preferred_element_type=jnp.float32)
        * score_scale
    )
    highest = jnp.max(scores, axis=3)
    weights = jnp.exp(scores - highest[..., None])
    totals = jnp.sum(weights, axis=3)
    summed = jnp.einsum(
        "jsgp,pjd->sjgd",
        weights.astype(jnp.bfloat16),
        prefix_values,
        preferred_element_type=jnp.float32,
    )
    prefix_out = (summed / jnp.transpose(totals, (1, 0, 2))[..., None]).astype(jnp.bfloat16)
    prefix_lse = jnp.transpose(highest + jnp.log(totals), (1, 0, 2))
    rows_here = suffix_cache.shape[1]
    flat_index = lax.axis_index("ctx") * lax.axis_size("smp") + lax.axis_index("smp")
    row_ids = lax.dynamic_slice_in_dim(cache_sample, flat_index * rows_here, rows_here, 0)
    local_ids = row_ids % group_rows
    row_queries = jnp.take(queries_split, local_ids, axis=0)
    row_lengths = jnp.take(suffix_length, local_ids, axis=0)
    suffix_out, suffix_lse = suffix_piece(
        row_queries, suffix_cache, row_lengths, key_value_heads_here, score_scale
    )
    onehot = (local_ids[None, :] == jnp.arange(group_rows, dtype=jnp.int32)[:, None]).astype(
        jnp.float32
    )
    present = jnp.sum(onehot, axis=1)[:, None]
    placed_out = jnp.dot(
        onehot,
        suffix_out.reshape(rows_here, -1).astype(jnp.float32),
        precision=lax.Precision.HIGHEST,
    )
    placed_lse = jnp.dot(
        onehot, suffix_lse.reshape(rows_here, heads_local), precision=lax.Precision.HIGHEST
    )
    own_lse = prefix_lse.reshape(group_rows, heads_local)
    other_lse = jnp.where(present > 0, placed_lse, own_lse)
    top = jnp.maximum(own_lse, other_lse)
    own_weight = jnp.exp(own_lse - top)
    other_weight = present * jnp.exp(other_lse - top)
    both_weight = own_weight + other_weight
    own_values = prefix_out.reshape(group_rows, heads_local, HD).astype(jnp.float32)
    other_values = placed_out.reshape(group_rows, heads_local, HD)
    local_out = (
        own_weight[..., None] * own_values + other_weight[..., None] * other_values
    ) / both_weight[..., None]
    local_lse = top + jnp.log(both_weight)
    attn_slice = merge_pieces(
        (
            lax.all_to_all(
                local_out.reshape(group_rows, 1, -1), "ctx", split_axis=2, concat_axis=1, tiled=True
            ),
            lax.all_to_all(
                local_lse.reshape(group_rows, 1, -1), "ctx", split_axis=2, concat_axis=1, tiled=True
            ),
        )
    )
    proj_weight = w_out[0]
    all_attn = lax.all_gather(attn_slice, "smp", axis=0, tiled=True)
    own_state = (
        residual.astype(jnp.float32)
        + lax.psum_scatter(
            jnp.dot(all_attn, proj_weight, preferred_element_type=jnp.float32),
            ("ctx", "head"),
            scatter_dimension=0,
            tiled=True,
        )
    ).astype(jnp.bfloat16)
    state = lax.all_gather(own_state, ("ctx", "head"), axis=0, tiled=True)
    state_wide = state.astype(jnp.float32)
    square_part = jnp.sum(state_wide * state_wide, axis=1)
    scaled = (state_wide * norm_gain).astype(jnp.bfloat16)
    gate_portion = jnp.dot(scaled, gate_matrix, preferred_element_type=jnp.float32)
    up_part = jnp.dot(scaled, w_up, preferred_element_type=jnp.float32)
    gate_sum, up_sum, square_sum = (
        lax.psum(gate_portion.astype(jnp.bfloat16), "smp").astype(jnp.float32),
        lax.psum(up_part.astype(jnp.bfloat16), "smp").astype(jnp.float32),
        lax.psum(square_part.astype(jnp.bfloat16), "smp").astype(jnp.float32),
    )
    activated = activate(gate_sum, up_sum, square_sum)
    ffn_rows = lax.psum_scatter(
        jnp.dot(activated, w_down, preferred_element_type=jnp.float32).astype(jnp.bfloat16),
        ("ctx", "head"),
        scatter_dimension=0,
        tiled=True,
    ).astype(jnp.float32)
    return (own_state.astype(jnp.float32) + ffn_rows).astype(jnp.bfloat16)


def solution(mesh):
    in_specs = (
        P(("group", "smp"), "head", None),
        P(None, ("group", "ctx"), "head", None),
        P(None, ("group", "ctx", "smp"), None, "head", None),
        P(("group", "smp")),
        P("group"),
        P(("group", "ctx", "head"), "smp"),
        P("head", "ctx", "smp"),
        P("smp"),
        P("smp", ("ctx", "head")),
        P("smp", ("ctx", "head")),
        P(("ctx", "head"), "smp"),
    )
    out_specs = P(("group", "ctx", "head"), "smp")
    return jax.shard_map(
        on_device, mesh=mesh, in_specs=in_specs, out_specs=out_specs, check_vma=False
    )
```

profile of v0, /device:TPU:0, one launch (start us, length us, event | category | flops | bytes accessed | tf_op | source)
XLA Modules:
  0.0 360.2 jit_solution(7161917489603728494)
XLA Ops:
  10.4 5.9 %fusion.46 = (bf16[1,32,128,1,512]{4,2,3,1,0:T(8,128)(2,1)}, bf16[1,32,128,1,512]{4,2,3,1,0:T(8,128)(2,1)}) fusion(bf16[2,32,128,1,512]{4,2,3,1,0:T(8,128)(2,1)} %param.13), kind=kLoop, calls=%fused_computation.77 | loop fusion | bytes 16777216 | tf_op jit(solution)/shard_map/slice | solution.py:16
  16.4 6.4 %copy.57 = bf16[1,32,128,1,512]{2,4,1,3,0:T(8,128)(2,1)} copy(bf16[1,32,128,1,512]{4,2,3,1,0:T(8,128)(2,1)} %get-tuple-element.18) | data formatting | bytes 8388608
  22.8 8.1 %multiply_reduce_fusion = (f32[4,128,8]{1,2,0:T(8,128)S(1)}, f32[4,128,8,1024]{3,1,2,0:T(8,128)}) fusion(bf16[1024,4,128,1]{0,2,3,1:T(8,128)(2,1)S(1)} %bitcast.92, bf16[128,4,8,128]{3,2,1,0:T(8,128)(2,1)S(1)} %bitcast.89), kind=kOutput, calls=%fused_computation.3 | convolution fusion | flops 1082126336 | bytes 18890752 | tf_op jit(solution)/shard_map/sjgd,pjd->jsgp/dot_general | solution.py:74
  32.2 3.5 fusion.48
  36.4 7.7 %fusion.1 = f32[4,128,8]{1,2,0:T(8,128)S(1)} fusion(f32[4,128,8,1024]{3,1,2,0:T(8,128)} %get-tuple-element.22, f32[4,128,8]{1,2,0:T(8,128)S(1)} %get-tuple-element.21), kind=kLoop, calls=%fused_computation.5 | loop fusion | flops 12578816 | bytes 16809984 | tf_op jit(solution)/shard_map/reduce_sum | solution.py:79
  44.9 6.3 %all-to-all-start = ((f32[128,1,32]{0,1,2:T(1,128)}), f32[128,1,32]{0,1,2:T(1,128)S(1)}, u32[]{:S(2)}, u32[]{:S(2)}) async-start(f32[128,1,32]{0,1,2:T(1,128)} %bitcast.8), calls=%async_computation | async-start | bytes 32768 | tf_op jit(solution)/shard_map/all_to_all | solution.py:126
  51.8 6.4 %copy.58 = bf16[1,32,128,1,512]{2,4,1,3,0:T(8,128)(2,1)} copy(bf16[1,32,128,1,512]{4,2,3,1,0:T(8,128)(2,1)} %get-tuple-element.17) | data formatting | bytes 8388608
  58.2 4.5 %fusion.18 = bf16[32,4,8,128]{3,2,1,0:T(8,128)(2,1)S(1)} fusion(bf16[32,128,4,128]{1,3,2,0:T(8,128)(2,1)} %bitcast.91, f32[32,4,8,128]{3,2,1,0:T(8,128)S(1)} %get-tuple-element.24, f32[32,4,8]{2,1,0:T(4,128)S(1)} %fusion.24, f32[32,4,8]{2,1,0:T(4,128)S(1)} %get-tuple-element.23), kind=kOutput, calls=%fused_computation.28 | convolution fusion | flops 34078720 | bytes 4988928 | tf_op jit(solution)/shard_map/rjgt,rtjd->rjgd/dot_general | solution.py:26
  62.7 7.6 %fusion.12 = bf16[128,4,8,128]{0,3,2,1:T(8,128)(2,1)S(1)} fusion(bf16[1024,4,128,1]{0,2,3,1:T(8,128)(2,1)S(1)} %bitcast.96, f32[4,128,8,1024]{3,1,2,0:T(8,128)} %get-tuple-element.22, f32[4,128,8]{1,2,0:T(8,128)S(1)} %get-tuple-element.21, f32[128,4,8]{0,2,1:T(8,128)S(1)} %bitcast.99), kind=kOutput, calls=%fused_computation.22 | convolution fusion | flops 1087373312 | bytes 18907136 | tf_op jit(solution)/shard_map/jsgp,pjd->sjgd/dot_general | solution.py:80
  70.3 2.0 fusion.11
  72.4 5.1 %all-to-all-start.1 = ((f32[128,1,4096]{0,1,2:T(1,128)}), f32[128,1,4096]{0,1,2:T(1,128)S(1)}, u32[]{:S(2)}, u32[]{:S(2)}) async-start(f32[128,1,4096]{0,1,2:T(1,128)} %bitcast.93), calls=%async_computation.1 | async-start | bytes 4194304 | tf_op jit(solution)/shard_map/all_to_all | solution.py:123
  77.5 47.6 %all-to-all-done.1 = f32[128,1,4096]{0,1,2:T(1,128)S(1)} async-done(((f32[128,1,4096]{0,1,2:T(1,128)}), f32[128,1,4096]{0,1,2:T(1,128)S(1)}, u32[]{:S(2)}, u32[]{:S(2)}) %all-to-all-start.1) | async-done | bytes 2097184 | tf_op jit(solution)/shard_map/all_to_all | solution.py:123
  125.4 8.2 %all_gather.6 = bf16[256,1024]{0,1:T(8,128)(2,1)S(1)} all-gather(bf16[128,1024]{0,1:T(8,128)(2,1)S(1)} %bitcast.94), channel_id=1, replica_groups=mesh['group'=2,'ctx'=4,'smp'=2,'head'=2] {'smp'}, dimensions={0}, use_global_device_ids=true | all-gather | bytes 786432 | tf_op jit(solution)/shard_map/all_gather | solution.py:132
  133.6 7.7 %fusion.4 = f32[256,4096]{1,0:T(8,128)} fusion(bf16[256,1024]{0,1:T(8,128)(2,1)S(1)} %all_gather.6, bf16[1,1024,4096]{2,1,0:T(8,128)(2,1)} %param.17), kind=kOutput, calls=%fused_computation.7 | convolution fusion | flops 2147483648 | bytes 13107200 | tf_op jit(solution)/shard_map/dot_general | solution.py:136
  141.4 48.2 %reduce-scatter.3.cloned.1.call-done = f32[32,4096]{1,0:T(8,128)} async-done(((f32[256,4096]{1,0:T(8,128)}), f32[32,4096]{1,0:T(8,128)}) %reduce-scatter.3.cloned.1.call-update) | async-done | bytes 524304 | tf_op jit(solution)/shard_map/reduce_scatter | solution.py:135
  189.6 1.8 add_convert_fusion.1
  191.5 27.7 %all-gather.2.cloned.1.call-done = bf16[256,4096]{1,0:T(8,128)(2,1)} async-done(((bf16[32,4096]{1,0:T(8,128)(2,1)}), bf16[256,4096]{1,0:T(8,128)(2,1)}) %all-gather.2.cloned.1.call-update) | async-done | bytes 2097168 | tf_op jit(solution)/shard_map/all_gather | solution.py:142
  219.2 12.0 %convolution_convert_fusion.1 = bf16[256,2048]{1,0:T(8,128)(2,1)} fusion(bf16[4096,2048]{1,0:T(8,128)(2,1)} %param.20, bf16[256,4096]{1,0:T(8,128)(2,1)} %all-gather.2.cloned.1.call-done, f32[4096]{0:T(1024)S(1)} %copy-done.6), kind=kOutput, calls=%fused_computation.16 | convolution fusion | flops 4298637312 | bytes 19939328 | tf_op jit(solution)/shard_map/dot_general | solution.py:147
  231.2 9.3 %convolution_convert_fusion.2 = bf16[256,2048]{1,0:T(8,128)(2,1)} fusion(bf16[4096,2048]{1,0:T(8,128)(2,1)} %param.19, bf16[256,4096]{1,0:T(8,128)(2,1)S(1)} %copy-done.3, f32[4096]{0:T(1024)S(1)} %copy-done.6), kind=kOutput, calls=%fused_computation.17 | convolution fusion | flops 4298637312 | bytes 19939328 | tf_op jit(solution)/shard_map/dot_general | solution.py:146
  241.1 5.2 %psum.21 = bf16[256]{0:T(256)(128)(2,1)S(1)} all-reduce(bf16[256]{0:T(256)(128)(2,1)S(1)} %fusion.8), channel_id=1, replica_groups=mesh['group'=2,'ctx'=4,'smp'=2,'head'=2] {'smp'}, use_global_device_ids=true, to_apply=%region_10.11 | all-reduce | flops 256 | bytes 1024 | tf_op jit(solution)/shard_map/psum | solution.py:151
  246.2 56.8 %all-reduce.3.cloned.1.call-done = (bf16[256,2048]{1,0:T(8,128)(2,1)}, bf16[256,2048]{1,0:T(8,128)(2,1)}) async-done(((bf16[256,2048]{1,0:T(8,128)(2,1)}, bf16[256,2048]{1,0:T(8,128)(2,1)}), (bf16[256,2048]{1,0:T(8,128)(2,1)}, bf16[256,2048]{1,0:T(8,128)(2,1)})) %all-reduce.3.cloned.1.call-update) | async-done | bytes 2097168 | tf_op jit(solution)/shard_map/psum | solution.py:150
  303.0 12.6 %convolution_convert_fusion = bf16[256,4096]{1,0:T(8,128)(2,1)} fusion(bf16[2048,4096]{1,0:T(8,128)(2,1)} %param.21, bf16[256,2048]{1,0:T(8,128)(2,1)} %get-tuple-element.5, bf16[256,2048]{1,0:T(8,128)(2,1)} %get-tuple-element.6, f32[256]{0:T(256)S(1)} %add_rsqrt_fusion), kind=kOutput, calls=%fused_computation.13 | convolution fusion | flops 4301258752 | bytes 20972544 | tf_op jit(solution)/shard_map/dot_general | solution.py:155
  315.7 36.3 %reduce-scatter.5.cloned.1.call-done = bf16[32,4096]{1,0:T(8,128)(2,1)} async-done(((bf16[256,4096]{1,0:T(8,128)(2,1)}), bf16[32,4096]{1,0:T(8,128)(2,1)}) %reduce-scatter.5.cloned.1.call-update) | async-done | bytes 262160 | tf_op jit(solution)/shard_map/reduce_scatter | solution.py:154
  352.0 1.7 add_convert_fusion
  (44 shorter events, 8.2 us)
Async XLA Ops:
  6.5 25.0 %copy-start = (s32[128]{0:T(128)S(1)}, s32[128]{0:T(128)}, u32[]{:S(2)}) copy-start(s32[128]{0:T(128)} %param.14) | copy-start | bytes 1540
  6.5 3.7 %copy-start.5 = (s32[256]{0:T(256)S(1)}, s32[256]{0:T(256)}, u32[]{:S(2)}) copy-start(s32[256]{0:T(256)} %param.15) | copy-start | bytes 3076
  44.9 27.5 %all-to-all-start = ((f32[128,1,32]{0,1,2:T(1,128)}), f32[128,1,32]{0,1,2:T(1,128)S(1)}, u32[]{:S(2)}, u32[]{:S(2)}) async-start(f32[128,1,32]{0,1,2:T(1,128)} %bitcast.8), calls=%async_computation | async-start | bytes 32768 | tf_op jit(solution)/shard_map/all_to_all | solution.py:126
  72.4 52.7 %all-to-all-start.1 = ((f32[128,1,4096]{0,1,2:T(1,128)}), f32[128,1,4096]{0,1,2:T(1,128)S(1)}, u32[]{:S(2)}, u32[]{:S(2)}) async-start(f32[128,1,4096]{0,1,2:T(1,128)} %bitcast.93), calls=%async_computation.1 | async-start | bytes 4194304 | tf_op jit(solution)/shard_map/all_to_all | solution.py:123
  77.5 112.2 %reduce-scatter.3.cloned.1.call-start = ((), (), s32[]{:S(2)}) async-start(), calls=%async_computation.4 | async-start | bytes 4718592 | tf_op jit(solution)/shard_map/reduce_scatter | solution.py:135
  141.3 48.3 %copy-start.4 = (bf16[32,4096]{1,0:T(8,128)(2,1)S(1)}, bf16[32,4096]{1,0:T(8,128)(2,1)}, u32[]{:S(2)}) copy-start(bf16[32,4096]{1,0:T(8,128)(2,1)} %param.16) | copy-start | bytes 786436
  141.3 77.9 %copy-start.6 = (f32[4096]{0:T(1024)S(1)}, f32[4096]{0:T(1024)}, u32[]{:S(2)}) copy-start(f32[4096]{0:T(1024)} %param.18) | copy-start | bytes 49156
  141.3 77.9 %all-gather.2.cloned.1.call-start = ((), (), s32[]{:S(2)}) async-start(), calls=%async_computation.5 | async-start | bytes 2359296 | tf_op jit(solution)/shard_map/all_gather | solution.py:142
  191.4 111.6 %all-reduce.3.cloned.1.call-start = ((), (), s32[]{:S(2)}) async-start(), calls=%async_computation.7 | async-start | bytes 4194304 | tf_op jit(solution)/shard_map/psum | solution.py:150
  219.2 12.0 %copy-start.3 = (bf16[256,4096]{1,0:T(8,128)(2,1)S(1)}, bf16[256,4096]{1,0:T(8,128)(2,1)}, u32[]{:S(2)}) copy-start(bf16[256,4096]{1,0:T(8,128)(2,1)} %all-gather.2.cloned.1.call-done) | copy-start | bytes 6291460
  240.5 111.4 %reduce-scatter.5.cloned.1.call-start = ((), (), s32[]{:S(2)}) async-start(), calls=%async_computation.6 | async-start | bytes 2359296 | tf_op jit(solution)/shard_map/reduce_scatter | solution.py:154
  303.0 48.9 %copy-start.2 = (bf16[32,4096]{1,0:T(8,128)(2,1)S(1)}, bf16[32,4096]{1,0:T(8,128)(2,1)}, u32[]{:S(2)}) copy-start(bf16[32,4096]{1,0:T(8,128)(2,1)} %add_convert_fusion.1) | copy-start | bytes 786436
  303.0 50.7 %copy-start.1 = (s32[128]{0:T(128)S(1)}, s32[128]{0:T(128)}, u32[]{:S(2)}) copy-start(s32[128]{0:T(128)} %param.14) | copy-start | bytes 1540
Sparse Core Ops, SparseCore 0:
  141.4 48.1 reduce-scatter.2
  191.6 27.6 all-gather.1
  240.6 62.3 all-reduce.2
  315.8 36.1 reduce-scatter.4
where the time goes:
time: 361 us; the launch traced here: 360 us
  waiting for transfers between devices  217 us (60%)
  matrix products  68.3 us (19%)
  local copies, waits for them, and re-layouts  24.4 us (7%)
  blocking collectives  13.4 us (4%)
  between operations  13.2 us (4%)
  other arithmetic  12.6 us (3%)
  starting transfers between devices  11.6 us (3%)
    psum x1, waiting for transfers between devices, on_device(): lax.psum(up_part.astype(jnp.bfloat16), 'smp').astype(jnp.float32)  56.8 us
    reduce_scatter x1, waiting for transfers between devices, on_device(): lax.psum_scatter(jnp.dot(all_attn, proj_weight, preferred_element_type=jn...  48.2 us
    all_to_all x1, waiting for transfers between devices, on_device(): lax.all_to_all(local_out.reshape(group_rows, 1, -1), 'ctx', split_axis=2,...  47.6 us
    reduce_scatter x1, waiting for transfers between devices, on_device(): lax.psum_scatter(jnp.dot(activated, w_down, preferred_element_type=jnp.fl...  36.3 us
    all_gather x1, waiting for transfers between devices, on_device(): state = lax.all_gather(own_state, ('ctx', 'head'), axis=0, tiled=True)  27.7 us
    unnamed x18, local copies, waits for them, and re-layouts  14.8 us
    dot_general x1, matrix products, on_device(): jnp.dot(activated, w_down, preferred_element_type=jnp.float32)  12.6 us
    dot_general x1, matrix products, on_device(): up_part = jnp.dot(scaled, w_up, preferred_element_type=jnp.float32)  12 us
  transfers between devices with their start and end apart: 6, of which 5 were waited for; matrix products, arithmetic and copies ran while one was open for 6% of the time, Pallas kernels for 0%

commit v1 on v0

--- a/solution.py
+++ b/solution.py
@@ -2,12 +2,20 @@
 import jax.numpy as jnp
 from jax import lax
 from jax.sharding import PartitionSpec as P
+from jax.lax import all_to_all, psum
 
 D = 8192
 QUERY_HEADS = 64
 KEY_VALUE_HEADS = 8
 HD = 128
 EPSILON = 1e-05
+
+
+def push_grid(row_data, ax_name):
+    return jnp.concatenate(
+        all_to_all(jnp.stack(jnp.split(row_data, psum(1, ax_name), axis=2), axis=0), ax_name, 0, 0),
+        axis=1,
+    )
 
 
 def suffix_piece(row_queries, suffix_cache, row_lengths, key_value_heads_here, score_scale):
@@ -120,9 +128,7 @@
     local_lse = top + jnp.log(both_weight)
     attn_slice = merge_pieces(
         (
-            lax.all_to_all(
-                local_out.reshape(group_rows, 1, -1), "ctx", split_axis=2, concat_axis=1, tiled=True
-            ),
+            push_grid(local_out.reshape(group_rows, 1, -1), "ctx"),
             lax.all_to_all(
                 local_lse.reshape(group_rows, 1, -1), "ctx", split_axis=2, concat_axis=1, tiled=True
             ),

time: 361 us -> 362 us (level)
  no operation moved by 1% of the time
where the time goes in v1:
time: 362 us; the launch traced here: 361 us
  waiting for transfers between devices  217 us (60%)
  matrix products  66.9 us (18%)
  local copies, waits for them, and re-layouts  24.7 us (7%)
  other arithmetic  14.2 us (4%)
  blocking collectives  13.4 us (4%)
  between operations  13.3 us (4%)
  starting transfers between devices  11.6 us (3%)
    psum x1, waiting for transfers between devices, on_device(): lax.psum(up_part.astype(jnp.bfloat16), 'smp').astype(jnp.float32)  56.8 us
    reduce_scatter x1, waiting for transfers between devices, on_device(): lax.psum_scatter(jnp.dot(all_attn, proj_weight, preferred_element_type=jn...  48.2 us
    all_to_all x1, waiting for transfers between devices, push_grid(): all_to_all(jnp.stack(jnp.split(row_data, psum(1, ax_name), axis=2), axis=...  47.6 us
    reduce_scatter x1, waiting for transfers between devices, on_device(): lax.psum_scatter(jnp.dot(activated, w_down, preferred_element_type=jnp.fl...  36.2 us
    all_gather x1, waiting for transfers between devices, on_device(): state = lax.all_gather(own_state, ('ctx', 'head'), axis=0, tiled=True)  27.7 us
    unnamed x18, local copies, waits for them, and re-layouts  14.8 us
    dot_general x1, matrix products, on_device(): jnp.dot(activated, w_down, preferred_element_type=jnp.float32)  12.6 us
    dot_general x1, matrix products, on_device(): up_part = jnp.dot(scaled, w_up, preferred_element_type=jnp.float32)  12 us
  transfers between devices with their start and end apart: 6, of which 5 were waited for; matrix products, arithmetic and copies ran while one was open for 6% of the time, Pallas kernels for 0%

profile of v1, /device:TPU:0, one launch (start us, length us, event | category | flops | bytes accessed | tf_op | source)
XLA Modules:
  0.0 360.7 jit_solution(5946010752161462324)
XLA Ops:
  6.5 1.7 fusion.49
  10.4 5.9 %fusion.48 = (bf16[1,32,128,1,512]{4,2,3,1,0:T(8,128)(2,1)}, bf16[1,32,128,1,512]{4,2,3,1,0:T(8,128)(2,1)}) fusion(bf16[2,32,128,1,512]{4,2,3,1,0:T(8,128)(2,1)} %param.13), kind=kLoop, calls=%fused_computation.84 | loop fusion | bytes 16777216 | tf_op jit(solution)/shard_map/slice | solution.py:24
  16.4 6.4 %copy.55 = bf16[1,32,128,1,512]{2,4,1,3,0:T(8,128)(2,1)} copy(bf16[1,32,128,1,512]{4,2,3,1,0:T(8,128)(2,1)} %get-tuple-element.18) | data formatting | bytes 8388608
  22.8 8.1 %multiply_reduce_fusion = (f32[4,128,8]{1,2,0:T(8,128)S(1)}, f32[4,128,8,1024]{3,1,2,0:T(8,128)}) fusion(bf16[1024,4,128,1]{0,2,3,1:T(8,128)(2,1)S(1)} %bitcast.107, bf16[128,4,8,128]{3,2,1,0:T(8,128)(2,1)S(1)} %bitcast.104), kind=kOutput, calls=%fused_computation.3 | convolution fusion | flops 1082126336 | bytes 18890752 | tf_op jit(solution)/shard_map/sjgd,pjd->jsgp/dot_general | solution.py:82
  32.2 3.5 fusion.50
  36.4 7.7 %fusion.1 = f32[4,128,8]{1,2,0:T(8,128)S(1)} fusion(f32[4,128,8,1024]{3,1,2,0:T(8,128)} %get-tuple-element.26, f32[4,128,8]{1,2,0:T(8,128)S(1)} %get-tuple-element.25), kind=kLoop, calls=%fused_computation.5 | loop fusion | flops 12578816 | bytes 16809984 | tf_op jit(solution)/shard_map/reduce_sum | solution.py:87
  44.9 6.3 %all-to-all-start = ((f32[128,1,32]{0,1,2:T(1,128)}), f32[128,1,32]{0,1,2:T(1,128)S(1)}, u32[]{:S(2)}, u32[]{:S(2)}) async-start(f32[128,1,32]{0,1,2:T(1,128)} %bitcast.8), calls=%async_computation | async-start | bytes 32768 | tf_op jit(solution)/shard_map/all_to_all | solution.py:132
  51.8 6.4 %copy.56 = bf16[1,32,128,1,512]{2,4,1,3,0:T(8,128)(2,1)} copy(bf16[1,32,128,1,512]{4,2,3,1,0:T(8,128)(2,1)} %get-tuple-element.17) | data formatting | bytes 8388608
  58.2 4.5 %fusion.19 = bf16[32,4,8,128]{3,2,1,0:T(8,128)(2,1)S(1)} fusion(bf16[32,128,4,128]{1,3,2,0:T(8,128)(2,1)} %bitcast.106, f32[32,4,8,128]{3,2,1,0:T(8,128)S(1)} %get-tuple-element.28, f32[32,4,8]{2,1,0:T(4,128)S(1)} %fusion.26, f32[32,4,8]{2,1,0:T(4,128)S(1)} %get-tuple-element.27), kind=kOutput, calls=%fused_computation.30 | convolution fusion | flops 34078720 | bytes 4988928 | tf_op jit(solution)/shard_map/rjgt,rtjd->rjgd/dot_general | solution.py:34
  62.7 7.6 %fusion.13 = bf16[128,4,8,128]{0,3,2,1:T(8,128)(2,1)S(1)} fusion(bf16[1024,4,128,1]{0,2,3,1:T(8,128)(2,1)S(1)} %bitcast.110, f32[4,128,8,1024]{3,1,2,0:T(8,128)} %get-tuple-element.26, f32[4,128,8]{1,2,0:T(8,128)S(1)} %get-tuple-element.25, f32[128,4,8]{0,2,1:T(8,128)S(1)} %bitcast.113), kind=kOutput, calls=%fused_computation.25 | convolution fusion | flops 1087373312 | bytes 18907136 | tf_op jit(solution)/shard_map/jsgp,pjd->sjgd/dot_general | solution.py:88
  72.6 5.1 %all-to-all-start.1 = ((f32[4,128,1,1024]{1,3,2,0:T(8,128)}), f32[4,128,1,1024]{1,3,2,0:T(8,128)S(1)}, u32[]{:S(2)}, u32[]{:S(2)}) async-start(f32[4,128,1,1024]{1,3,2,0:T(8,128)} %pad_maximum_fusion), calls=%async_computation.1 | async-start | bytes 4194304 | tf_op jit(solution)/shard_map/all_to_all | solution.py:16
  77.8 47.6 %all-to-all-done.1 = f32[4,128,1,1024]{1,3,2,0:T(8,128)S(1)} async-done(((f32[4,128,1,1024]{1,3,2,0:T(8,128)}), f32[4,128,1,1024]{1,3,2,0:T(8,128)S(1)}, u32[]{:S(2)}, u32[]{:S(2)}) %all-to-all-start.1) | async-done | bytes 2097184 | tf_op jit(solution)/shard_map/all_to_all | solution.py:16
  125.9 8.2 %all_gather.6 = bf16[256,1024]{0,1:T(8,128)(2,1)S(1)} all-gather(bf16[128,1024]{0,1:T(8,128)(2,1)S(1)} %fusion.24), channel_id=1, replica_groups=mesh['group'=2,'ctx'=4,'smp'=2,'head'=2] {'smp'}, dimensions={0}, use_global_device_ids=true | all-gather | bytes 786432 | tf_op jit(solution)/shard_map/all_gather | solution.py:138
  134.1 7.7 %fusion.4 = f32[256,4096]{1,0:T(8,128)} fusion(bf16[256,1024]{0,1:T(8,128)(2,1)S(1)} %all_gather.6, bf16[1,1024,4096]{2,1,0:T(8,128)(2,1)} %param.17), kind=kOutput, calls=%fused_computation.7 | convolution fusion | flops 2147483648 | bytes 13107200 | tf_op jit(solution)/shard_map/dot_general | solution.py:142
  141.9 48.2 %reduce-scatter.3.cloned.1.call-done = f32[32,4096]{1,0:T(8,128)} async-done(((f32[256,4096]{1,0:T(8,128)}), f32[32,4096]{1,0:T(8,128)}) %reduce-scatter.3.cloned.1.call-update) | async-done | bytes 524304 | tf_op jit(solution)/shard_map/reduce_scatter | solution.py:141
  190.1 1.8 add_convert_fusion.1
  192.0 27.7 %all-gather.2.cloned.1.call-done = bf16[256,4096]{1,0:T(8,128)(2,1)} async-done(((bf16[32,4096]{1,0:T(8,128)(2,1)}), bf16[256,4096]{1,0:T(8,128)(2,1)}) %all-gather.2.cloned.1.call-update) | async-done | bytes 2097168 | tf_op jit(solution)/shard_map/all_gather | solution.py:148
  219.7 12.0 %convolution_convert_fusion.1 = bf16[256,2048]{1,0:T(8,128)(2,1)} fusion(bf16[4096,2048]{1,0:T(8,128)(2,1)} %param.20, bf16[256,4096]{1,0:T(8,128)(2,1)} %all-gather.2.cloned.1.call-done, f32[4096]{0:T(1024)S(1)} %copy-done.6), kind=kOutput, calls=%fused_computation.16 | convolution fusion | flops 4298637312 | bytes 19939328 | tf_op jit(solution)/shard_map/dot_general | solution.py:153
  231.7 9.3 %convolution_convert_fusion.2 = bf16[256,2048]{1,0:T(8,128)(2,1)} fusion(bf16[4096,2048]{1,0:T(8,128)(2,1)} %param.19, bf16[256,4096]{1,0:T(8,128)(2,1)S(1)} %copy-done.3, f32[4096]{0:T(1024)S(1)} %copy-done.6), kind=kOutput, calls=%fused_computation.17 | convolution fusion | flops 4298637312 | bytes 19939328 | tf_op jit(solution)/shard_map/dot_general | solution.py:152
  241.6 5.2 %psum.21 = bf16[256]{0:T(256)(128)(2,1)S(1)} all-reduce(bf16[256]{0:T(256)(128)(2,1)S(1)} %fusion.8), channel_id=1, replica_groups=mesh['group'=2,'ctx'=4,'smp'=2,'head'=2] {'smp'}, use_global_device_ids=true, to_apply=%region_10.11 | all-reduce | flops 256 | bytes 1024 | tf_op jit(solution)/shard_map/psum | solution.py:157
  246.7 56.8 %all-reduce.3.cloned.1.call-done = (bf16[256,2048]{1,0:T(8,128)(2,1)}, bf16[256,2048]{1,0:T(8,128)(2,1)}) async-done(((bf16[256,2048]{1,0:T(8,128)(2,1)}, bf16[256,2048]{1,0:T(8,128)(2,1)}), (bf16[256,2048]{1,0:T(8,128)(2,1)}, bf16[256,2048]{1,0:T(8,128)(2,1)})) %all-reduce.3.cloned.1.call-update) | async-done | bytes 2097168 | tf_op jit(solution)/shard_map/psum | solution.py:156
  303.6 12.6 %convolution_convert_fusion = bf16[256,4096]{1,0:T(8,128)(2,1)} fusion(bf16[2048,4096]{1,0:T(8,128)(2,1)} %param.21, bf16[256,2048]{1,0:T(8,128)(2,1)} %get-tuple-element.5, bf16[256,2048]{1,0:T(8,128)(2,1)} %get-tuple-element.6, f32[256]{0:T(256)S(1)} %add_rsqrt_fusion), kind=kOutput, calls=%fused_computation.13 | convolution fusion | flops 4301258752 | bytes 20972544 | tf_op jit(solution)/shard_map/dot_general | solution.py:161
  316.2 36.2 %reduce-scatter.5.cloned.1.call-done = bf16[32,4096]{1,0:T(8,128)(2,1)} async-done(((bf16[256,4096]{1,0:T(8,128)(2,1)}), bf16[32,4096]{1,0:T(8,128)(2,1)}) %reduce-scatter.5.cloned.1.call-update) | async-done | bytes 262160 | tf_op jit(solution)/shard_map/reduce_scatter | solution.py:160
  352.4 1.7 add_convert_fusion
  (47 shorter events, 9.0 us)
Async XLA Ops:
  6.5 25.0 %copy-start = (s32[128]{0:T(128)S(1)}, s32[128]{0:T(128)}, u32[]{:S(2)}) copy-start(s32[128]{0:T(128)} %param.14) | copy-start | bytes 1540
  6.5 3.7 %copy-start.5 = (s32[256]{0:T(256)S(1)}, s32[256]{0:T(256)}, u32[]{:S(2)}) copy-start(s32[256]{0:T(256)} %param.15) | copy-start | bytes 3076
  44.9 27.8 %all-to-all-start = ((f32[128,1,32]{0,1,2:T(1,128)}), f32[128,1,32]{0,1,2:T(1,128)S(1)}, u32[]{:S(2)}, u32[]{:S(2)}) async-start(f32[128,1,32]{0,1,2:T(1,128)} %bitcast.8), calls=%async_computation | async-start | bytes 32768 | tf_op jit(solution)/shard_map/all_to_all | solution.py:132
  72.6 52.7 %all-to-all-start.1 = ((f32[4,128,1,1024]{1,3,2,0:T(8,128)}), f32[4,128,1,1024]{1,3,2,0:T(8,128)S(1)}, u32[]{:S(2)}, u32[]{:S(2)}) async-start(f32[4,128,1,1024]{1,3,2,0:T(8,128)} %pad_maximum_fusion), calls=%async_computation.1 | async-start | bytes 4194304 | tf_op jit(solution)/shard_map/all_to_all | solution.py:16
  77.7 112.4 %reduce-scatter.3.cloned.1.call-start = ((), (), s32[]{:S(2)}) async-start(), calls=%async_computation.4 | async-start | bytes 4718592 | tf_op jit(solution)/shard_map/reduce_scatter | solution.py:141
  141.8 48.3 %copy-start.4 = (bf16[32,4096]{1,0:T(8,128)(2,1)S(1)}, bf16[32,4096]{1,0:T(8,128)(2,1)}, u32[]{:S(2)}) copy-start(bf16[32,4096]{1,0:T(8,128)(2,1)} %param.16) | copy-start | bytes 786436
  141.8 77.9 %copy-start.6 = (f32[4096]{0:T(1024)S(1)}, f32[4096]{0:T(1024)}, u32[]{:S(2)}) copy-start(f32[4096]{0:T(1024)} %param.18) | copy-start | bytes 49156
  141.8 77.9 %all-gather.2.cloned.1.call-start = ((), (), s32[]{:S(2)}) async-start(), calls=%async_computation.5 | async-start | bytes 2359296 | tf_op jit(solution)/shard_map/all_gather | solution.py:148
  191.9 111.6 %all-reduce.3.cloned.1.call-start = ((), (), s32[]{:S(2)}) async-start(), calls=%async_computation.7 | async-start | bytes 4194304 | tf_op jit(solution)/shard_map/psum | solution.py:156
  219.7 12.0 %copy-start.3 = (bf16[256,4096]{1,0:T(8,128)(2,1)S(1)}, bf16[256,4096]{1,0:T(8,128)(2,1)}, u32[]{:S(2)}) copy-start(bf16[256,4096]{1,0:T(8,128)(2,1)} %all-gather.2.cloned.1.call-done) | copy-start | bytes 6291460
  241.0 111.4 %reduce-scatter.5.cloned.1.call-start = ((), (), s32[]{:S(2)}) async-start(), calls=%async_computation.6 | async-start | bytes 2359296 | tf_op jit(solution)/shard_map/reduce_scatter | solution.py:160
  303.5 48.9 %copy-start.2 = (bf16[32,4096]{1,0:T(8,128)(2,1)S(1)}, bf16[32,4096]{1,0:T(8,128)(2,1)}, u32[]{:S(2)}) copy-start(bf16[32,4096]{1,0:T(8,128)(2,1)} %add_convert_fusion.1) | copy-start | bytes 786436
  303.6 50.6 %copy-start.1 = (s32[128]{0:T(128)S(1)}, s32[128]{0:T(128)}, u32[]{:S(2)}) copy-start(s32[128]{0:T(128)} %param.14) | copy-start | bytes 1540
Sparse Core Ops, SparseCore 0:
  141.9 48.1 reduce-scatter.2
  192.1 27.6 all-gather.1
  241.1 62.3 all-reduce.2
  316.3 36.0 reduce-scatter.4
